TPU v7x, 256 devices: a whole 4x4x8 slice. The times are simulated.
256 devices in a mesh: layer: 4 (over y_lo, core), phi: 64 (over y_hi, z, x).
Axes of the slice: x: 4, y: 4 (y_hi: 2, y_lo: 2; y = y_hi * 2 + y_lo), z: 8, core: 2. Of those that a mesh axis runs over, the one named last changes fastest.
Arguments:
- hit_features: bfloat16 [4, 64, 1024, 128], P('layer', 'phi'), may hold values from -6 to 6
- edge_features: bfloat16 [4, 64, 4, 1024, 128], P('layer', 'phi'), may hold values from -6 to 6
- sender_slot: int32 [4, 64, 4, 1024], P('layer', 'phi'), may hold values from 0 to 1023
- receiver_slot: int32 [4, 64, 4, 1024], P('layer', 'phi'), may hold values from 0 to 1023
- edge_count: int32 [4, 64, 4], P('layer', 'phi'), may hold values from 0 to 1024, as said below
- grad_hits: bfloat16 [4, 64, 1024, 128], P('layer', 'phi'), may hold values from -6 to 6
- grad_edges: bfloat16 [4, 64, 4, 1024, 128], P('layer', 'phi'), may hold values from -6 to 6
- w_edge_in: bfloat16 [384, 128], replicated, may hold values from -0.3125 to 0.3125
- w_edge_out: bfloat16 [128, 128], replicated, may hold values from -0.5 to 0.5
- w_node_in: bfloat16 [256, 128], replicated, may hold values from -0.375 to 0.375
- w_node_out: bfloat16 [128, 128], replicated, may hold values from -0.5 to 0.5
Outputs:
- hit_grads: float32 [4, 64, 1024, 128], P('layer', 'phi')
- edge_grads: bfloat16 [4, 64, 4, 1024, 128], P('layer', 'phi')
- edge_in_grad: float32 [384, 128], replicated
- edge_out_grad: float32 [128, 128], replicated
- node_in_grad: float32 [256, 128], replicated
- node_out_grad: float32 [128, 128], replicated
Inputs may be any that keep to these rules, and one draw needn't show every extreme that they name: `edge_count`: live slots come first in each block. Kind 0 edges have their sender in the same shard, kind 1 in the previous layer group, kind 2 in the previous phi sector, kind 3 in the next one (phi closes into a loop). Kind 1 has no live slots in layer group 0. Some block is full in every draw. `sender_slot`: rows of dead slots are arbitrary. `receiver_slot`: rows of dead slots are arbitrary.
All inputs are finite; a program needn't handle non-finite values.
Results may differ from a plain program's by a relative error of at most 0.009.
Values may be sent and summed in bfloat16 or wider, within the bound.
A program may use at most 64 MiB of HBM per device.

v0:
```python
import jax
import jax.numpy as jnp
from jax import lax
from jax.sharding import PartitionSpec as P

norm_eps = 1e-05


def passed_along(value, axis, steps):
    count = lax.axis_size(axis)
    initial, last = (max(0, -steps), min(count, count - steps))
    return lax.ppermute(value, axis, [(source, source + steps) for source in range(initial, last)])


def passed_along_2(block, axis, distance):
    devices = range(lax.axis_size(axis))
    route = [((i - distance) % len(devices), i) for i in devices]
    return lax.ppermute(block, axis, route)


def norm_act(pre_act):
    average = jnp.mean(pre_act, axis=-1, keepdims=True)
    centred = pre_act - average
    spread = jnp.mean(centred * centred, axis=-1, keepdims=True)
    scaled = centred * lax.rsqrt(spread + norm_eps)
    return scaled * jax.nn.sigmoid(scaled)


def norm_act_back(pre_act, upstream):
    _, pullback = jax.vjp(norm_act, pre_act)
    return pullback(upstream)[0]


def one_hot_rows(indices, node_total):
    return (indices[:, None] == lax.iota(jnp.int32, node_total)[None, :]).astype(jnp.bfloat16)


def pick_rows(selector, table):
    return jnp.dot(selector, table, preferred_element_type=jnp.float32)


def split_parts(values):
    upper = values.astype(jnp.bfloat16)
    lower = (values - upper.astype(jnp.float32)).astype(jnp.bfloat16)
    return (upper, lower)


def add_rows(selector, values):
    upper, lower = split_parts(values)
    dims = (((0,), (0,)), ((), ()))
    first = lax.dot_general(selector, upper, dims, preferred_element_type=jnp.float32)
    second = lax.dot_general(selector, lower, dims, preferred_element_type=jnp.float32)
    return first + second


def body(
    hit_features,
    edge_features,
    sender_slot,
    receiver_slot,
    edge_count,
    grad_hits,
    grad_edges,
    w_edge_in,
    w_edge_out,
    w_node_in,
    w_node_out,
):
    local_rows = hit_features[0, 0]
    node_total = local_rows.shape[0]
    features = local_rows.shape[1]
    send_all = sender_slot[0, 0]
    recv_all = receiver_slot[0, 0]
    counts = edge_count[0, 0]
    edge_all = edge_features[0, 0]
    grad_edge_all = grad_edges[0, 0]
    grad_local = grad_hits[0, 0]
    kind_total = send_all.shape[0]
    capacity = send_all.shape[1]
    tile_rows = 256
    tile_total = capacity // tile_rows
    lower_rows = passed_along(local_rows, "layer", 1)
    prev_rows = passed_along_2(local_rows, "phi", 1)
    next_rows = passed_along_2(local_rows, "phi", -1)
    sources = (local_rows, lower_rows, prev_rows, next_rows)
    positions = lax.iota(jnp.int32, capacity)
    live_all = (positions[None, :] < counts[:, None]).astype(jnp.float32)

    def tile_indices(k, offset):
        send_idx = lax.dynamic_slice_in_dim(send_all[k], offset, tile_rows, 0)
        recv_idx = lax.dynamic_slice_in_dim(recv_all[k], offset, tile_rows, 0)
        live_mask = lax.dynamic_slice_in_dim(live_all[k], offset, tile_rows, 0)
        return (send_idx, recv_idx, live_mask)

    def forward_tile(k, offset, send_hot, recv_hot):
        edge_rows = lax.dynamic_slice_in_dim(edge_all[k], offset, tile_rows, 0)
        sender_rows = pick_rows(send_hot, sources[k]).astype(jnp.bfloat16)
        receiver_rows = pick_rows(recv_hot, local_rows).astype(jnp.bfloat16)
        inputs = jnp.concatenate([sender_rows, receiver_rows, edge_rows], axis=-1)
        pre_act = jnp.dot(inputs, w_edge_in, preferred_element_type=jnp.float32)
        hidden = norm_act(pre_act).astype(jnp.bfloat16)
        return (inputs, pre_act, hidden)

    def run_tiles(tile_step, totals):

        def looped(number, inner):
            return tile_step(number * tile_rows, inner)

        return lax.fori_loop(0, tile_total, looped, totals)

    incoming = jnp.zeros((node_total, features), jnp.float32)
    stored = []
    for k in range(kind_total):

        def message_step(offset, totals):
            total, kept = totals
            send_idx, recv_idx, live_mask = tile_indices(k, offset)
            send_hot = one_hot_rows(send_idx, node_total)
            recv_hot = one_hot_rows(recv_idx, node_total)
            inputs, pre_act, hidden = forward_tile(k, offset, send_hot, recv_hot)
            message = (
                jnp.dot(hidden, w_edge_out, preferred_element_type=jnp.float32) * live_mask[:, None]
            )
            total = total + add_rows(recv_hot, message)
            kept = (
                lax.dynamic_update_slice_in_dim(kept[0], inputs, offset, 0),
                lax.dynamic_update_slice_in_dim(kept[1], pre_act, offset, 0),
                lax.dynamic_update_slice_in_dim(kept[2], hidden, offset, 0),
            )
            return (total, kept)

        kept_start = (
            jnp.zeros((capacity, 3 * features), jnp.bfloat16),
            jnp.zeros((capacity, features), jnp.float32),
            jnp.zeros((capacity, features), jnp.bfloat16),
        )
        incoming, kept_done = run_tiles(message_step, (incoming, kept_start))
        stored.append(kept_done)
    incoming = incoming.astype(jnp.bfloat16)
    node_in = jnp.concatenate([local_rows, incoming], axis=-1)
    node_pre = jnp.dot(node_in, w_node_in, preferred_element_type=jnp.float32)
    node_hidden = norm_act(node_pre).astype(jnp.bfloat16)
    node_hidden_grad = jnp.dot(grad_local, w_node_out.T, preferred_element_type=jnp.float32)
    node_out_part = jnp.dot(node_hidden.T, grad_local, preferred_element_type=jnp.float32)
    node_pre_grad = norm_act_back(node_pre, node_hidden_grad).astype(jnp.bfloat16)
    node_input_grad = jnp.dot(node_pre_grad, w_node_in.T, preferred_element_type=jnp.float32)
    node_in_part = jnp.dot(node_in.T, node_pre_grad, preferred_element_type=jnp.float32)
    incoming_upper, incoming_lower = split_parts(node_input_grad[:, features:])
    recv_total = jnp.zeros((node_total, features), jnp.float32)
    in_total = jnp.zeros((3 * features, features), jnp.float32)
    out_total = jnp.zeros((features, features), jnp.float32)
    send_parts = []
    edge_parts = []
    for k in range(kind_total):

        def back_step(offset, totals):
            recv_sum, send_sum, in_sum, out_sum, edge_done = totals
            send_idx, recv_idx, live_mask = tile_indices(k, offset)
            send_hot = one_hot_rows(send_idx, node_total)
            recv_hot = one_hot_rows(recv_idx, node_total)
            inputs = lax.dynamic_slice_in_dim(stored[k][0], offset, tile_rows, 0)
            pre_act = lax.dynamic_slice_in_dim(stored[k][1], offset, tile_rows, 0)
            hidden = lax.dynamic_slice_in_dim(stored[k][2], offset, tile_rows, 0)
            grad_rows = lax.dynamic_slice_in_dim(grad_edge_all[k], offset, tile_rows, 0)
            picked = pick_rows(recv_hot, incoming_upper) + pick_rows(recv_hot, incoming_lower)
            message_grad = (live_mask[:, None] * (grad_rows.astype(jnp.float32) + picked)).astype(
                jnp.bfloat16
            )
            hidden_grad = jnp.dot(message_grad, w_edge_out.T, preferred_element_type=jnp.float32)
            pre_grad = norm_act_back(pre_act, hidden_grad).astype(jnp.bfloat16)
            input_grad = jnp.dot(pre_grad, w_edge_in.T, preferred_element_type=jnp.float32)
            edge_new = (grad_rows.astype(jnp.float32) + input_grad[:, 2 * features :]).astype(
                jnp.bfloat16
            )
            edge_done = lax.dynamic_update_slice_in_dim(edge_done, edge_new, offset, 0)
            recv_sum = recv_sum + add_rows(recv_hot, input_grad[:, features : 2 * features])
            send_sum = send_sum + add_rows(send_hot, input_grad[:, :features])
            in_sum = in_sum + jnp.dot(inputs.T, pre_grad, preferred_element_type=jnp.float32)
            out_sum = out_sum + jnp.dot(hidden.T, message_grad, preferred_element_type=jnp.float32)
            return (recv_sum, send_sum, in_sum, out_sum, edge_done)

        start_totals = (
            recv_total,
            jnp.zeros((node_total, features), jnp.float32),
            in_total,
            out_total,
            grad_edge_all[k],
        )
        recv_total, send_sum, in_total, out_total, edge_done = run_tiles(back_step, start_totals)
        send_parts.append(send_sum)
        edge_parts.append(edge_done)
    from_upper = passed_along(send_parts[1].astype(jnp.bfloat16), "layer", -1).astype(jnp.float32)
    from_next = passed_along_2(send_parts[2].astype(jnp.bfloat16), "phi", -1).astype(jnp.float32)
    from_prev = passed_along_2(send_parts[3].astype(jnp.bfloat16), "phi", 1).astype(jnp.float32)
    returned = from_next + from_prev
    hit_total = (
        grad_local.astype(jnp.float32)
        + node_input_grad[:, :features]
        + recv_total
        + send_parts[0]
        + from_upper
        + returned
    )
    summed = lax.psum((in_total, out_total, node_in_part, node_out_part), ("layer", "phi"))
    shard_count = lax.axis_size("layer") * lax.axis_size("phi")
    edge_stack = jnp.stack(edge_parts)
    return (
        hit_total[None, None],
        edge_stack[None, None],
        summed[0] / shard_count,
        summed[1] / shard_count,
        summed[2] / shard_count,
        summed[3] / shard_count,
    )


def solution(mesh):
    placed = (
        P("layer", "phi", None, None),
        P("layer", "phi", None, None, None),
        P("layer", "phi", None, None),
        P("layer", "phi", None, None),
        P("layer", "phi", None),
        P("layer", "phi", None, None),
        P("layer", "phi", None, None, None),
        P(),
        P(),
        P(),
        P(),
    )
    return jax.shard_map(
        body,
        mesh=mesh,
        in_specs=placed,
        out_specs=(
            P("layer", "phi", None, None),
            P("layer", "phi", None, None, None),
            P(),
            P(),
            P(),
            P(),
        ),
        check_vma=False,
    )
```

profile of v0, /device:TPU:2, one launch (start us, length us, event | category | flops | bytes accessed | tf_op | source)
XLA Modules:
  0.0 593.0 jit_solution(756839716940063795)
XLA Ops:
  7.2 2.4 collective-permute-start
  9.7 1.5 collective-permute-start.1
  12.4 1.5 copy.17
  16.6 33.2 %while.168 = (s32[]{:T(128)}, f32[1024,128]{1,0:T(8,128)S(1)}, bf16[1024,384]{0,1:T(8,128)(2,1)}, f32[1024,128]{0,1:T(8,128)}, bf16[1024,128]{0,1:T(8,128)(2,1)S...) while((s32[]{:T(128)}, f32[1024,128]{1,0:T(8,128)S(1)}, ...), condition=%wide.region_3.0_spmd.clone, body=%wide.region_0.0_spmd.clone.sunk | while | flops 305463552 | bytes 8575457 | solution.py:109
  16.7 1.4 convolution_convert_fusion.22
  54.2 26.9 %while.165 = (s32[]{:T(128)}, f32[1024,128]{1,0:T(8,128)S(1)}, bf16[1024,384]{0,1:T(8,128)(2,1)}, f32[1024,128]{0,1:T(8,128)}, bf16[1024,128]{0,1:T(8,128)(2,1)}...) while((s32[]{:T(128)}, f32[1024,128]{1,0:T(8,128)S(1)}, ...), condition=%wide.region_7.0_spmd, body=%wide.region_4.0_spmd.sunk | while | flops 305332480 | bytes 5421311 | solution.py:109
  83.7 27.0 %while.166 = (s32[]{:T(128)}, f32[1024,128]{1,0:T(8,128)S(1)}, bf16[1024,384]{0,1:T(8,128)(2,1)}, f32[1024,128]{0,1:T(8,128)}, bf16[1024,128]{0,1:T(8,128)(2,1)}...) while((s32[]{:T(128)}, f32[1024,128]{1,0:T(8,128)S(1)}, ...), condition=%wide.region_11.0_spmd, body=%wide.region_8.0_spmd.sunk | while | flops 305332480 | bytes 5421311 | solution.py:109
  113.3 27.0 %while.167 = (s32[]{:T(128)}, f32[1024,128]{1,0:T(8,128)S(1)}, bf16[1024,384]{0,1:T(8,128)(2,1)}, f32[1024,128]{0,1:T(8,128)}, bf16[1024,128]{0,1:T(8,128)(2,1)}...) while((s32[]{:T(128)}, f32[1024,128]{1,0:T(8,128)S(1)}, ...), condition=%wide.region_15.0_spmd, body=%wide.region_12.0_spmd.sunk | while | flops 305332480 | bytes 5421311 | solution.py:109
  144.1 1.9 fusion.147
  148.2 51.9 %while.169 = (s32[]{:T(128)}, f32[1024,128]{1,0:T(8,128)S(1)}, f32[1024,128]{1,0:T(8,128)}, f32[384,128]{1,0:T(8,128)S(1)}, f32[128,128]{1,0:T(8,128)S(1)}, /*in...) while((s32[]{:T(128)}, f32[1024,128]{1,0:T(8,128)S(1)}, ...), condition=%wide.region_25.26_spmd.clone, body=%wide.region_20.25_spmd.clone.sunk | while | flops 473990912 | bytes 11069784 | solution.py:109
  167.1 2.4 fusion.376
  180.4 2.4 fusion.376
  193.6 2.4 fusion.376
  200.1 40.0 %while.170 = (s32[]{:T(128)}, f32[1024,128]{1,0:T(8,128)S(1)}, f32[1024,128]{1,0:T(8,128)}, f32[384,128]{1,0:T(8,128)S(1)}, f32[128,128]{1,0:T(8,128)S(1)}, /*in...) while((s32[]{:T(128)}, f32[1024,128]{1,0:T(8,128)S(1)}, ...), condition=%wide.region_31.0_spmd.clone, body=%wide.region_26.31_spmd.clone.sunk | while | flops 473794304 | bytes 13166961 | solution.py:109
  213.1 2.4 fusion.394
  223.4 2.4 fusion.394
  233.6 2.4 fusion.394
  240.1 39.9 %while.171 = (s32[]{:T(128)}, f32[1024,128]{1,0:T(8,128)S(1)}, f32[1024,128]{1,0:T(8,128)}, f32[384,128]{1,0:T(8,128)S(1)}, f32[128,128]{1,0:T(8,128)S(1)}, /*in...) while((s32[]{:T(128)}, f32[1024,128]{1,0:T(8,128)S(1)}, ...), condition=%wide.region_37.38_spmd.clone, body=%wide.region_32.37_spmd.clone.sunk | while | flops 473794304 | bytes 13166961 | solution.py:109
  253.1 2.4 fusion.412
  263.3 2.4 fusion.412
  273.6 2.4 fusion.412
  280.1 39.9 %while.172 = (s32[]{:T(128)}, f32[1024,128]{1,0:T(8,128)S(1)}, f32[1024,128]{1,0:T(8,128)}, f32[384,128]{1,0:T(8,128)S(1)}, f32[128,128]{1,0:T(8,128)S(1)}, /*in...) while((s32[]{:T(128)}, f32[1024,128]{1,0:T(8,128)S(1)}, ...), condition=%wide.region_43.44_spmd.clone, body=%wide.region_38.43_spmd.clone.sunk | while | flops 473794304 | bytes 13166961 | solution.py:109
  293.0 2.4 fusion.430
  303.2 2.4 fusion.430
  313.5 2.4 fusion.430
  320.7 1.8 convert_element_type.565
  322.4 1.5 collective-permute-start.5
  324.7 7.7 %collective-permute-start.4 = (bf16[1024,128]{1,0:T(8,128)(2,1)}, bf16[1024,128]{1,0:T(8,128)(2,1)S(1)}, u32[]{:S(2)}, u32[]{:S(2)}) collective-permute-start(bf16[1024,128]{1,0:T(8,128)(2,1)} %convert_element_type.563), channel_id=1, source_target_pairs={{1,0},{2,1},{3,2},{4,3},{5,4},{6,5},{7,6},{8,7},{9,8},{10,9},{11,1... | collective-permute-start | bytes 786440 | tf_op jit(solution)/shard_map/ppermute | solution.py:18
  335.6 244.9 %all-reduce.3.cloned.1.call-done = (f32[384,128]{1,0:T(8,128)}, f32[128,128]{1,0:T(8,128)}, f32[256,128]{1,0:T(8,128)}, f32[128,128]{1,0:T(8,128)}) async-done(((f32[384,128]{1,0:T(8,128)}, f32[128,128]{1,0:T(8,128)}, f32[256,128]{1,0:T(8,128)}, f32[128,128]{1,0:T(8,128)}), (f32[384,128]{1,0:T(8,128)}, f32[128,128]{1,0:T(8,128)}, f32[256,128]{1,0:T(8,128)}, ...) | async-done | bytes 458768 | tf_op jit(solution)/shard_map/psum | solution.py:204
  580.4 1.6 broadcast_multiply_fusion.9
  582.0 1.5 broadcast_multiply_fusion.10
  583.5 1.7 broadcast_multiply_fusion.8
  (938 shorter events, 276.4 us)
Async XLA Ops:
  7.2 133.1 %copy-start = (bf16[256,128]{1,0:T(8,128)(2,1)S(1)}, bf16[256,128]{1,0:T(8,128)(2,1)}, u32[]{:S(2)}) copy-start(bf16[256,128]{1,0:T(8,128)(2,1)} %param.36) | copy-start | bytes 196612
  7.2 573.2 %all-reduce.3.cloned.1.call-start = ((), (), s32[]{:S(2)}) async-start(), calls=%async_computation | async-start | bytes 917504 | tf_op jit(solution)/shard_map/psum | solution.py:204
  7.2 44.3 %collective-permute-start = (bf16[1024,128]{1,0:T(8,128)(2,1)}, bf16[1024,128]{1,0:T(8,128)(2,1)}, u32[]{:S(2)}, u32[]{:S(2)}) collective-permute-start(bf16[1024,128]{1,0:T(8,128)(2,1)} %bitcast.13), channel_id=1, source_target_pairs={{0,64},{64,128},{128,192},{1,65},{65,129},{129,193},{2,66},{66,130... | collective-permute-start | bytes 786440 | tf_op jit(solution)/shard_map/ppermute | solution.py:12
  9.7 71.4 %collective-permute-start.1 = (bf16[1024,128]{1,0:T(8,128)(2,1)}, bf16[1024,128]{1,0:T(8,128)(2,1)}, u32[]{:S(2)}, u32[]{:S(2)}) collective-permute-start(bf16[1024,128]{1,0:T(8,128)(2,1)} %bitcast.13), channel_id=1, source_target_pairs={{63,0},{0,1},{1,2},{2,3},{3,4},{4,5},{5,6},{6,7},{7,8},{8,9},{9,10... | collective-permute-start | bytes 786440 | tf_op jit(solution)/shard_map/ppermute | solution.py:18
  11.2 99.5 %collective-permute-start.2 = (bf16[1024,128]{1,0:T(8,128)(2,1)}, bf16[1024,128]{1,0:T(8,128)(2,1)}, u32[]{:S(2)}, u32[]{:S(2)}) collective-permute-start(bf16[1024,128]{1,0:T(8,128)(2,1)} %bitcast.13), channel_id=1, source_target_pairs={{1,0},{2,1},{3,2},{4,3},{5,4},{6,5},{7,6},{8,7},{9,8},{10,9},{11,1... | collective-permute-start | bytes 786440 | tf_op jit(solution)/shard_map/ppermute | solution.py:18
  16.6 33.9 %copy-start.3 = (bf16[1,1,4,1024,128]{4,3,2,1,0:T(8,128)(2,1)S(1)}, bf16[1,1,4,1024,128]{4,3,2,1,0:T(8,128)(2,1)}, u32[]{:S(2)}) copy-start(bf16[1,1,4,1024,128]{4,3,2,1,0:T(8,128)(2,1)} %param.33) | copy-start | bytes 3145732
  16.7 5.4 copy-start.37
  25.0 5.4 copy-start.37
  33.3 5.4 copy-start.37
  41.6 5.4 copy-start.37
  200.1 1.5 copy-start.31
  219.6 1.5 copy-start.31
  229.9 1.5 copy-start.31
  240.1 1.5 copy-start.33
  249.3 1.5 copy-start.33
  259.6 1.5 copy-start.33
  269.8 1.5 copy-start.33
  289.3 1.5 copy-start.35
  299.5 1.5 copy-start.35
  309.7 1.5 copy-start.35
  320.0 3.9 copy-start.6
  322.4 9.9 %copy-start.7 = (f32[1024,128]{1,0:T(8,128)S(1)}, f32[1024,128]{1,0:T(8,128)}, u32[]{:S(2)}) copy-start(f32[1024,128]{1,0:T(8,128)} %get-tuple-element.1998) | copy-start | bytes 1572868
  322.4 262.7 %collective-permute-start.5 = (bf16[1024,128]{1,0:T(8,128)(2,1)}, bf16[1024,128]{1,0:T(8,128)(2,1)S(1)}, u32[]{:S(2)}, u32[]{:S(2)}) collective-permute-start(bf16[1024,128]{1,0:T(8,128)(2,1)} %convert_element_type.565), channel_id=1, source_target_pairs={{63,0},{0,1},{1,2},{2,3},{3,4},{4,5},{5,6},{6,7},{7,8},{8,9},{9,10... | collective-permute-start | bytes 786440 | tf_op jit(solution)/shard_map/ppermute | solution.py:18
  323.9 10.5 %copy-start.26 = (bf16[1024,128]{1,0:T(8,128)(2,1)S(1)}, bf16[1024,128]{1,0:T(8,128)(2,1)}, u32[]{:S(2)}) copy-start(bf16[1024,128]{1,0:T(8,128)(2,1)} %get-tuple-element.2001) | copy-start | bytes 786436
  324.7 260.5 %collective-permute-start.4 = (bf16[1024,128]{1,0:T(8,128)(2,1)}, bf16[1024,128]{1,0:T(8,128)(2,1)S(1)}, u32[]{:S(2)}, u32[]{:S(2)}) collective-permute-start(bf16[1024,128]{1,0:T(8,128)(2,1)} %convert_element_type.563), channel_id=1, source_target_pairs={{1,0},{2,1},{3,2},{4,3},{5,4},{6,5},{7,6},{8,7},{9,8},{10,9},{11,1... | collective-permute-start | bytes 786440 | tf_op jit(solution)/shard_map/ppermute | solution.py:18
  332.4 2.0 copy-start.23
  332.4 2.0 copy-start.24
  332.4 2.1 copy-start.25
  333.1 252.1 %collective-permute-start.3 = (bf16[1024,128]{1,0:T(8,128)(2,1)}, bf16[1024,128]{1,0:T(8,128)(2,1)S(1)}, u32[]{:S(2)}, u32[]{:S(2)}) collective-permute-start(bf16[1024,128]{1,0:T(8,128)(2,1)} %convert_element_type.561), channel_id=1, source_target_pairs={{64,0},{128,64},{192,128},{65,1},{129,65},{193,129},{66,2},{130,66... | collective-permute-start | bytes 786440 | tf_op jit(solution)/shard_map/ppermute | solution.py:12
  334.4 250.7 %copy-start.13 = (f32[1024,256]{1,0:T(8,128)S(1)}, f32[1024,256]{1,0:T(8,128)}, u32[]{:S(2)}) copy-start(f32[1024,256]{1,0:T(8,128)} %copy-done.12) | copy-start | bytes 3145732
  335.6 249.6 %copy-start.8 = (f32[1024,128]{1,0:T(8,128)S(1)}, f32[1024,128]{1,0:T(8,128)}, u32[]{:S(2)}) copy-start(f32[1024,128]{1,0:T(8,128)} %get-tuple-element.1997) | copy-start | bytes 1572868
  583.5 1.7 copy-start.28
  (90 other events, 84.9 us)
Sparse Core Ops, SparseCore 0:
  320.8 259.5 all-reduce.2
where the time goes:
time: 598 us; the launch traced here: 593 us
  waiting for transfers between devices  245 us (41%)
  matrix products  212 us (35%)
  other arithmetic  66.8 us (11%)
  local copies, waits for them, and re-layouts  36.3 us (6%)
  starting transfers between devices  15 us (3%)
  between operations  14.3 us (2%)
    psum x1, waiting for transfers between devices, body(): lax.psum((in_total, out_total, node_in_part, node_out_part), ('layer', 'p...  245 us
    dot_general x64, matrix products, pick_rows(): return jnp.dot(selector, table, preferred_element_type=jnp.float32)  71.2 us
    dot_general x48, matrix products, add_rows(): lax.dot_general(selector, lower, dims, preferred_element_type=jnp.float32)  55.7 us
    dot_general x48, matrix products, add_rows(): lax.dot_general(selector, upper, dims, preferred_element_type=jnp.float32)  26.7 us
    dot_general x16, matrix products, back_step(): jnp.dot(inputs.T, pre_grad, preferred_element_type=jnp.float32)  18.4 us
    while x184, local copies, waits for them, and re-layouts  17.3 us
    dot_general x16, matrix products, back_step(): jnp.dot(hidden.T, message_grad, preferred_element_type=jnp.float32)  16.4 us
  transfers between devices with their start and end apart: 7, of which 1 were waited for; matrix products, arithmetic and copies ran while one was open for 16% of the time, Pallas kernels for 0%

commit v1 on v0

--- a/solution.py
+++ b/solution.py
@@ -201,7 +201,7 @@
         + from_upper
         + returned
     )
-    summed = lax.psum((in_total, out_total, node_in_part, node_out_part), ("layer", "phi"))
+    summed = lax.psum(lax.psum((in_total, out_total, node_in_part, node_out_part), "layer"), "phi")
     shard_count = lax.axis_size("layer") * lax.axis_size("phi")
     edge_stack = jnp.stack(edge_parts)
     return (

time: 598 us -> 1090 us (1.82)
  waiting for transfers between devices: 245 us -> 720 us
  local copies, waits for them, and re-layouts: 36.3 us -> 66.5 us
  matrix products: 212 us -> 190 us
    psum x1 -> x2, waiting for transfers between devices: 245 us -> 720 us  [the longest x1 684 us: body(): lax.psum(lax.psum((in_total, out_total, node_in_part, node_out_part), 'la...]
    while x184 -> x376, local copies, waits for them, and re-layouts: 17.3 us -> 47.2 us
    dot_general x64, matrix products: 71.2 us -> 47.4 us  [pick_rows(): return jnp.dot(selector, table, preferred_element_type=jnp.float32)]
  transfers between devices with their start and end apart: 7 -> 8, of which waited for: 1 -> 2; matrix products, arithmetic and copies ran while one was open for 16% -> 9% of each run, Pallas kernels for 0% -> 0%
where the time goes in v1:
time: 1090 us; the launch traced here: 1080 us
  waiting for transfers between devices  720 us (66%)
  matrix products  190 us (17%)
  other arithmetic  69 us (6%)
  local copies, waits for them, and re-layouts  66.5 us (6%)
  starting transfers between devices  15.2 us (1%)
  between operations  14.3 us (1%)
    psum x1, waiting for transfers between devices, body(): lax.psum(lax.psum((in_total, out_total, node_in_part, node_out_part), 'la...  684 us
    dot_general x48, matrix products, add_rows(): lax.dot_general(selector, lower, dims, preferred_element_type=jnp.float32)  59.6 us
    dot_general x64, matrix products, pick_rows(): return jnp.dot(selector, table, preferred_element_type=jnp.float32)  47.4 us
    while x376, local copies, waits for them, and re-layouts  47.2 us
    psum x1, waiting for transfers between devices, body(): lax.psum((in_total, out_total, node_in_part, node_out_part), 'layer')  36.2 us
    dot_general x48, matrix products, add_rows(): lax.dot_general(selector, upper, dims, preferred_element_type=jnp.float32)  26.7 us
  transfers between devices with their start and end apart: 8, of which 2 were waited for; matrix products, arithmetic and copies ran while one was open for 9% of the time, Pallas kernels for 0%

profile of v1, /device:TPU:2, one launch (start us, length us, event | category | flops | bytes accessed | tf_op | source)
XLA Modules:
  0.0 1079.4 jit_solution(3383421439632286404)
XLA Ops:
  7.2 2.5 collective-permute-start
  9.7 1.5 collective-permute-start.1
  16.7 31.7 %while.168 = (s32[]{:T(128)}, f32[1024,128]{1,0:T(8,128)S(1)}, bf16[1024,384]{0,1:T(8,128)(2,1)}, f32[1024,128]{0,1:T(8,128)}, bf16[1024,128]{0,1:T(8,128)(2,1)}...) while((s32[]{:T(128)}, f32[1024,128]{1,0:T(8,128)S(1)}, ...), condition=%wide.region_3.0_spmd.clone, body=%wide.region_0.0_spmd.clone.sunk | while | flops 305463552 | bytes 8051185 | solution.py:109
  22.0 1.7 fusion.358
  29.9 1.7 fusion.358
  37.8 1.7 fusion.358
  45.8 1.7 fusion.358
  52.1 27.0 %while.165 = (s32[]{:T(128)}, f32[1024,128]{1,0:T(8,128)S(1)}, bf16[1024,384]{0,1:T(8,128)(2,1)}, f32[1024,128]{0,1:T(8,128)}, bf16[1024,128]{0,1:T(8,128)(2,1)}...) while((s32[]{:T(128)}, f32[1024,128]{1,0:T(8,128)S(1)}, ...), condition=%wide.region_7.0_spmd, body=%wide.region_4.0_spmd.sunk | while | flops 305332480 | bytes 5421311 | solution.py:109
  81.7 27.0 %while.166 = (s32[]{:T(128)}, f32[1024,128]{1,0:T(8,128)S(1)}, bf16[1024,384]{0,1:T(8,128)(2,1)}, f32[1024,128]{0,1:T(8,128)}, bf16[1024,128]{0,1:T(8,128)(2,1)}...) while((s32[]{:T(128)}, f32[1024,128]{1,0:T(8,128)S(1)}, ...), condition=%wide.region_11.0_spmd, body=%wide.region_8.0_spmd.sunk | while | flops 305332480 | bytes 5421311 | solution.py:109
  111.3 27.0 %while.167 = (s32[]{:T(128)}, f32[1024,128]{1,0:T(8,128)S(1)}, bf16[1024,384]{0,1:T(8,128)(2,1)}, f32[1024,128]{0,1:T(8,128)}, bf16[1024,128]{0,1:T(8,128)(2,1)}...) while((s32[]{:T(128)}, f32[1024,128]{1,0:T(8,128)S(1)}, ...), condition=%wide.region_15.0_spmd, body=%wide.region_12.0_spmd.sunk | while | flops 305332480 | bytes 5421311 | solution.py:109
  144.5 55.4 %while.169 = (s32[]{:T(128)}, f32[1024,128]{1,0:T(8,128)S(1)}, f32[1024,128]{1,0:T(8,128)}, f32[384,128]{1,0:T(8,128)S(1)}, f32[128,128]{1,0:T(8,128)S(1)}, /*in...) while((s32[]{:T(128)}, f32[1024,128]{1,0:T(8,128)S(1)}, ...), condition=%wide.region_25.26_spmd.clone, body=%wide.region_20.25_spmd.clone.sunk | while | flops 473990912 | bytes 12265984 | solution.py:109
  165.1 2.4 fusion.376
  179.2 2.4 fusion.376
  193.3 2.4 fusion.376
  199.9 43.7 %while.170 = (s32[]{:T(128)}, f32[1024,128]{1,0:T(8,128)S(1)}, f32[1024,128]{1,0:T(8,128)}, f32[384,128]{1,0:T(8,128)S(1)}, f32[128,128]{1,0:T(8,128)S(1)}, /*in...) while((s32[]{:T(128)}, f32[1024,128]{1,0:T(8,128)S(1)}, ...), condition=%wide.region_31.0_spmd.clone, body=%wide.region_26.31_spmd.clone.sunk | while | flops 473794304 | bytes 14363161 | solution.py:109
  214.7 2.4 fusion.394
  225.9 2.4 fusion.394
  237.1 2.4 fusion.394
  243.6 43.7 %while.171 = (s32[]{:T(128)}, f32[1024,128]{1,0:T(8,128)S(1)}, f32[1024,128]{1,0:T(8,128)}, f32[384,128]{1,0:T(8,128)S(1)}, f32[128,128]{1,0:T(8,128)S(1)}, /*in...) while((s32[]{:T(128)}, f32[1024,128]{1,0:T(8,128)S(1)}, ...), condition=%wide.region_37.38_spmd.clone, body=%wide.region_32.37_spmd.clone.sunk | while | flops 473794304 | bytes 14363161 | solution.py:109
  258.4 2.4 fusion.412
  269.6 2.4 fusion.412
  280.8 2.4 fusion.412
  287.3 43.7 %while.172 = (s32[]{:T(128)}, f32[1024,128]{1,0:T(8,128)S(1)}, f32[1024,128]{1,0:T(8,128)}, f32[384,128]{1,0:T(8,128)S(1)}, f32[128,128]{1,0:T(8,128)S(1)}, /*in...) while((s32[]{:T(128)}, f32[1024,128]{1,0:T(8,128)S(1)}, ...), condition=%wide.region_43.44_spmd.clone, body=%wide.region_38.43_spmd.clone.sunk | while | flops 473794304 | bytes 14363161 | solution.py:109
  302.1 2.4 fusion.430
  313.2 2.4 fusion.430
  324.4 2.4 fusion.430
  331.7 1.8 convert_element_type.565
  335.7 7.7 collective-permute-start.4
  345.6 36.2 %all-reduce.7.cloned.1.call-done = (f32[384,128]{1,0:T(8,128)}, f32[128,128]{1,0:T(8,128)}, f32[256,128]{1,0:T(8,128)}, f32[128,128]{1,0:T(8,128)}) async-done(((f32[384,128]{1,0:T(8,128)}, f32[128,128]{1,0:T(8,128)}, f32[256,128]{1,0:T(8,128)}, f32[128,128]{1,0:T(8,128)}), (f32[384,128]{1,0:T(8,128)}, f32[128,128]{1,0:T(8,128)}, f32[256,128]{1,0:T(8,128)}, ...) | async-done | bytes 458768 | tf_op jit(solution)/shard_map/psum | solution.py:204
  383.6 2.1 fusion.146
  385.7 683.6 %all-reduce.5.cloned.1.call-done = (f32[384,128]{1,0:T(8,128)}, f32[128,128]{1,0:T(8,128)}, f32[256,128]{1,0:T(8,128)}, f32[128,128]{1,0:T(8,128)}) async-done(((f32[384,128]{1,0:T(8,128)}, f32[128,128]{1,0:T(8,128)}, f32[256,128]{1,0:T(8,128)}, f32[128,128]{1,0:T(8,128)}), (f32[384,128]{1,0:T(8,128)}, f32[128,128]{1,0:T(8,128)}, f32[256,128]{1,0:T(8,128)}, ...) | async-done | bytes 458768 | tf_op jit(solution)/shard_map/psum | solution.py:204
  1069.3 1.7 broadcast_multiply_fusion.8
  (1141 shorter events, 287.8 us)
Async XLA Ops:
  7.2 131.1 %copy-start = (bf16[256,128]{1,0:T(8,128)(2,1)S(1)}, bf16[256,128]{1,0:T(8,128)(2,1)}, u32[]{:S(2)}) copy-start(bf16[256,128]{1,0:T(8,128)(2,1)} %param.36) | copy-start | bytes 196612
  7.2 374.6 %all-reduce.7.cloned.1.call-start = ((), (), s32[]{:S(2)}) async-start(), calls=%async_computation.1 | async-start | bytes 917504 | tf_op jit(solution)/shard_map/psum | solution.py:204
  7.2 42.2 %collective-permute-start = (bf16[1024,128]{1,0:T(8,128)(2,1)}, bf16[1024,128]{1,0:T(8,128)(2,1)}, u32[]{:S(2)}, u32[]{:S(2)}) collective-permute-start(bf16[1024,128]{1,0:T(8,128)(2,1)} %bitcast.285), channel_id=1, source_target_pairs={{0,64},{64,128},{128,192},{1,65},{65,129},{129,193},{2,66},{66,130... | collective-permute-start | bytes 786440 | tf_op jit(solution)/shard_map/ppermute | solution.py:12
  9.7 69.4 %collective-permute-start.1 = (bf16[1024,128]{1,0:T(8,128)(2,1)}, bf16[1024,128]{1,0:T(8,128)(2,1)}, u32[]{:S(2)}, u32[]{:S(2)}) collective-permute-start(bf16[1024,128]{1,0:T(8,128)(2,1)} %bitcast.286), channel_id=1, source_target_pairs={{63,0},{0,1},{1,2},{2,3},{3,4},{4,5},{5,6},{6,7},{7,8},{8,9},{9,10... | collective-permute-start | bytes 786440 | tf_op jit(solution)/shard_map/ppermute | solution.py:18
  11.2 97.6 %collective-permute-start.2 = (bf16[1024,128]{1,0:T(8,128)(2,1)}, bf16[1024,128]{1,0:T(8,128)(2,1)}, u32[]{:S(2)}, u32[]{:S(2)}) collective-permute-start(bf16[1024,128]{1,0:T(8,128)(2,1)} %bitcast.287), channel_id=1, source_target_pairs={{1,0},{2,1},{3,2},{4,3},{5,4},{6,5},{7,6},{8,7},{9,8},{10,9},{11,1... | collective-permute-start | bytes 786440 | tf_op jit(solution)/shard_map/ppermute | solution.py:18
  16.7 31.7 %copy-start.3 = (bf16[1,1,4,1024,128]{4,3,2,1,0:T(8,128)(2,1)S(1)}, bf16[1,1,4,1024,128]{4,3,2,1,0:T(8,128)(2,1)}, u32[]{:S(2)}) copy-start(bf16[1,1,4,1024,128]{4,3,2,1,0:T(8,128)(2,1)} %param.33) | copy-start | bytes 3145732
  16.7 3.4 copy-start.58
  24.7 3.4 copy-start.58
  32.6 3.3 copy-start.58
  40.5 3.4 copy-start.58
  144.5 6.3 copy-start.50
  157.6 6.3 copy-start.50
  171.7 6.3 copy-start.50
  185.8 6.3 copy-start.50
  200.0 3.3 copy-start.52
  210.1 3.3 copy-start.52
  232.5 3.3 copy-start.52
  253.8 3.3 copy-start.54
  276.2 3.3 copy-start.54
  287.4 3.3 copy-start.56
  297.5 3.3 copy-start.56
  319.8 3.3 copy-start.56
  330.9 4.0 copy-start.6
  331.6 737.7 %all-reduce.5.cloned.1.call-start = ((), (), s32[]{:S(2)}) async-start(), calls=%async_computation | async-start | bytes 917504 | tf_op jit(solution)/shard_map/psum | solution.py:204
  333.5 9.9 copy-start.7
  333.5 49.5 %collective-permute-start.5 = (bf16[1024,128]{1,0:T(8,128)(2,1)}, bf16[1024,128]{1,0:T(8,128)(2,1)}, u32[]{:S(2)}, u32[]{:S(2)}) collective-permute-start(bf16[1024,128]{1,0:T(8,128)(2,1)} %convert_element_type.565), channel_id=1, source_target_pairs={{63,0},{0,1},{1,2},{2,3},{3,4},{4,5},{5,6},{6,7},{7,8},{8,9},{9,10... | collective-permute-start | bytes 786440 | tf_op jit(solution)/shard_map/ppermute | solution.py:18
  335.7 47.3 %collective-permute-start.4 = (bf16[1024,128]{1,0:T(8,128)(2,1)}, bf16[1024,128]{1,0:T(8,128)(2,1)}, u32[]{:S(2)}, u32[]{:S(2)}) collective-permute-start(bf16[1024,128]{1,0:T(8,128)(2,1)} %convert_element_type.563), channel_id=1, source_target_pairs={{1,0},{2,1},{3,2},{4,3},{5,4},{6,5},{7,6},{8,7},{9,8},{10,9},{11,1... | collective-permute-start | bytes 786440 | tf_op jit(solution)/shard_map/ppermute | solution.py:18
  343.4 38.4 %copy-start.22 = (bf16[1024,128]{1,0:T(8,128)(2,1)S(1)}, bf16[1024,128]{1,0:T(8,128)(2,1)}, u32[]{:S(2)}) copy-start(bf16[1024,128]{1,0:T(8,128)(2,1)} %get-tuple-element.2003) | copy-start | bytes 786436
  343.4 38.4 %copy-start.23 = (bf16[1024,128]{1,0:T(8,128)(2,1)S(1)}, bf16[1024,128]{1,0:T(8,128)(2,1)}, u32[]{:S(2)}) copy-start(bf16[1024,128]{1,0:T(8,128)(2,1)} %get-tuple-element.2002) | copy-start | bytes 786436
  343.4 38.4 %copy-start.24 = (bf16[1024,128]{1,0:T(8,128)(2,1)S(1)}, bf16[1024,128]{1,0:T(8,128)(2,1)}, u32[]{:S(2)}) copy-start(bf16[1024,128]{1,0:T(8,128)(2,1)} %get-tuple-element.2001) | copy-start | bytes 786436
  344.1 37.7 %copy-start.21 = (bf16[1024,128]{1,0:T(8,128)(2,1)S(1)}, bf16[1024,128]{1,0:T(8,128)(2,1)}, u32[]{:S(2)}) copy-start(bf16[1024,128]{1,0:T(8,128)(2,1)} %get-tuple-element.2004) | copy-start | bytes 786436
  344.1 38.8 %collective-permute-start.3 = (bf16[1024,128]{1,0:T(8,128)(2,1)}, bf16[1024,128]{1,0:T(8,128)(2,1)}, u32[]{:S(2)}, u32[]{:S(2)}) collective-permute-start(bf16[1024,128]{1,0:T(8,128)(2,1)} %convert_element_type.561), channel_id=1, source_target_pairs={{64,0},{128,64},{192,128},{65,1},{129,65},{193,129},{66,2},{130,66... | collective-permute-start | bytes 786440 | tf_op jit(solution)/shard_map/ppermute | solution.py:12
  (191 other events, 202.1 us)
Sparse Core Ops, SparseCore 0:
  331.8 49.9 all-reduce.6
  384.6 684.6 all-reduce.4
